TPU v7x, 512 devices: a whole 4x4x16 slice. The times are simulated.
512 devices in a mesh: kx: 16 (over z_hi, x), ky: 32 (over y, z_lo, core).
Axes of the slice: x: 4, y: 4, z: 16 (z_hi: 4, z_lo: 4; z = z_hi * 4 + z_lo), core: 2. Of those that a mesh axis runs over, the one named last changes fastest.
Arguments:
- states: bfloat16 [512, 4096, 128], P(('kx', 'ky')), may hold values from -6 to 6
- energies: bfloat16 [512, 128], P(('kx', 'ky')), may hold values from -2 to 2
- external: float32 [1, 4096], replicated, may hold values from -6 to 6
- reorder: int32 [2, 512, 4096], P(None, ('kx', 'ky')), may hold values from 0 to 4095, each once within a row
Outputs:
- band_response: float32 [512, 2, 1, 128, 128], P(('kx', 'ky'))
- density: float32 [2, 1, 4096], replicated
Inputs may be any that keep to these rules, and one draw needn't show every extreme that they name: Each row reorder[q, k] is a permutation of the 4096 grid components.
All inputs are finite; a program needn't handle non-finite values.
Results may differ from a plain program's by a relative error of at most 0.0029.
Values may be sent and summed in bfloat16 or wider, within the bound.
No kernel may reach another device: no remote copies, remote signals or barrier semaphores. Data moves between devices by JAX's collectives and lax.ppermute only.
A program may use at most 64 MiB of HBM per device.

v0:
```python
import math

import jax
import jax.numpy as jnp
import numpy as np
from jax import lax
from jax.experimental import pallas as pl
from jax.experimental.pallas import tpu as pltpu
from jax.sharding import Mesh, PartitionSpec as P


AXES = ("zh", "x", "y", "zl", "core")
AXIS_SIZES = (4, 4, 4, 4, 2)
KX = ("zh", "x")
KY = ("y", "zl", "core")
PLANE = ("x", "y", "core")
COLUMN = ("zh", "zl")

GX = 64
GY = 64
NQ = 2
GRID = GX * GY
BANDS = 128
LANES = 128
ROWS = GRID // LANES
STEP = 512
LIMIT = 24 * 1024 * 1024

SMEAR = 0.5
FERMI = 0.0
SCREEN = 4.0


def hartley_table(length):
    positions = np.arange(length)
    angles = positions[:, None] * positions[None, :] % length * (2.0 * math.pi / length)
    return (np.cos(angles) + np.sin(angles)) / math.sqrt(length)


def screening(len_x, len_y):
    freq_x = np.arange(len_x)
    freq_x = np.minimum(freq_x, len_x - freq_x)
    freq_y = np.arange(len_y)
    freq_y = np.minimum(freq_y, len_y - freq_y)
    return 1.0 / (1.0 + (freq_x[:, None] ** 2 + freq_y[None, :] ** 2) / SCREEN)


def lane_block(index):
    return pl.ds(pl.multiple_of(index * LANES, LANES), LANES)


def in_parts(value):
    high = value.astype(jnp.bfloat16)
    rest = value - high.astype(jnp.float32)
    middle = rest.astype(jnp.bfloat16)
    low = (rest - middle.astype(jnp.float32)).astype(jnp.bfloat16)
    return (high, middle, low)


def occupation(energy):
    return 1.0 / (1.0 + jnp.exp((energy - FERMI) / SMEAR))


def across(row):
    return jnp.broadcast_to(row, (BANDS, BANDS)).T


def weights(energy, far_energy):
    energy = energy.astype(jnp.float32)
    far_energy = far_energy.astype(jnp.float32)
    gap = far_energy - across(energy)
    filled = across(occupation(energy)) - occupation(far_energy)
    return filled * gap / (gap * gap + SMEAR * SMEAR)


def weigh(potential_ref, own_ref, weighted_ref):
    for block in range(ROWS):
        at = slice(block * LANES, (block + 1) * LANES)
        product = potential_ref[block : block + 1, :] * own_ref[:, at].astype(jnp.float32)
        weighted_ref[:, at] = product.astype(jnp.bfloat16)


def respond(weighted_ref, far_ref, own_ref, weight, terms_ref):
    points = math.prod(AXIS_SIZES)
    bands = jnp.zeros((BANDS, BANDS), jnp.float32)
    for start in range(0, GRID, STEP):
        at = slice(start, start + STEP)
        bands += jnp.dot(weighted_ref[:, at], far_ref[at, :], preferred_element_type=jnp.float32)
    response = weight * (bands * (1.0 / math.sqrt(GRID)))
    low = response.astype(jnp.bfloat16)
    for start in range(0, GRID, STEP):
        at = slice(start, start + STEP)
        orbitals = lax.dot_general(
            low, far_ref[at, :], (((1,), (1,)), ((), ())), preferred_element_type=jnp.float32
        )
        term = jnp.sum(own_ref[:, at].astype(jnp.float32) * orbitals, axis=0, keepdims=True)
        term = term * (1.0 / math.sqrt(BANDS * points))
        for block in range(STEP // LANES):
            row = start // LANES + block
            terms_ref[row : row + 1, :] = term[:, block * LANES : (block + 1) * LANES]
    return response


def mark_columns(order_ref, column_ref):
    columns = lax.broadcasted_iota(jnp.int32, (LANES, LANES), 0)
    for block in range(ROWS):
        mine = (order_ref[block : block + 1, :] % LANES) == columns
        column_ref[:, block * LANES : (block + 1) * LANES] = jnp.where(mine, 1.0, 0.0).astype(jnp.bfloat16)


def to_far_order(value_ref, order_ref, column_ref, parts_ref):
    parts = in_parts(value_ref[...])
    rows = lax.broadcasted_iota(jnp.int32, (ROWS, LANES), 0)
    for block in range(ROWS):
        mine = (order_ref[block : block + 1, :] // LANES) == rows
        at = slice(block * LANES, (block + 1) * LANES)
        for index, part in enumerate(parts):
            wide = part[block : block + 1, :].astype(jnp.float32)
            parts_ref[index * ROWS : (index + 1) * ROWS, at] = jnp.where(mine, wide, 0.0).astype(jnp.bfloat16)
    sums = lax.dot_general(
        parts_ref[...], column_ref[...], (((1,), (1,)), ((), ())), preferred_element_type=jnp.float32
    )
    return sums[:ROWS] + sums[ROWS : 2 * ROWS] + sums[2 * ROWS :]


def from_far_order(value, order_ref, column_ref, out_ref, first_row):
    stacked = jnp.concatenate([part.astype(jnp.float32) for part in in_parts(value)]).astype(jnp.bfloat16)
    rows = lax.broadcasted_iota(jnp.int32, (ROWS, LANES), 0)
    for start in range(0, GRID, STEP):
        at = slice(start, start + STEP)
        spread = jnp.dot(stacked, column_ref[:, at], preferred_element_type=jnp.float32)
        spread = spread[:ROWS] + spread[ROWS : 2 * ROWS] + spread[2 * ROWS :]
        for block in range(STEP // LANES):
            row = start // LANES + block
            mine = (order_ref[row : row + 1, :] // LANES) == rows
            picked = jnp.where(mine, spread[:, block * LANES : (block + 1) * LANES], 0.0)
            out_ref[first_row + row : first_row + row + 1, :] = jnp.sum(picked, axis=0, keepdims=True)


UNROLL = 32


def started(sems, *pairs, first=0):
    copies = []
    for index, (source, target) in enumerate(pairs):
        copies.append(pltpu.make_async_copy(source, target, sems.at[first + index]))
        copies[-1].start()
    return copies


def finished(copies):
    for copy in copies:
        copy.wait()


def prepare_kernel(order_smem, own_ref, order_ref, external_ref,
                   turned_ref, moved_ref, potential_ref, turned_out, moved_out,
                   wide, scattered, parts, column, sems):
    wide[...] = own_ref[...].astype(jnp.float32)

    def move(step, carry):
        base = step * UNROLL
        for offset in range(UNROLL):
            row = base + offset
            scattered[pl.ds(order_smem[row], 1), :] = wide[pl.ds(row, 1), :]
        return carry

    lax.fori_loop(0, GRID // UNROLL, move, 0)

    def turn(block, carry):
        at = lane_block(block)
        turned_ref[:, at] = wide[at, :].T.astype(jnp.bfloat16)
        moved_ref[:, at] = scattered[at, :].T.astype(jnp.bfloat16)
        return carry

    lax.fori_loop(0, ROWS, turn, 0)
    copies = started(sems, (turned_ref, turned_out), (moved_ref, moved_out))
    mark_columns(order_ref, column)
    potential_ref[...] = to_far_order(external_ref, order_ref, column, parts)
    finished(copies)


def second_kernel(order_smem, sent_ref, turned_ref, external_ref, energy_ref, far_energy_ref,
                  far_out, terms_ref, wide, gathered, weighted, far_ref, sems):
    wide[...] = sent_ref[...].astype(jnp.float32)

    def move(step, carry):
        base = step * UNROLL
        for offset in range(UNROLL):
            row = base + offset
            gathered[pl.ds(row, 1), :] = wide[pl.ds(order_smem[row], 1), :]
        return carry

    lax.fori_loop(0, GRID // UNROLL, move, 0)
    far_ref[...] = gathered[...].astype(jnp.bfloat16)
    stores = started(sems, (far_ref, far_out))
    weigh(external_ref, turned_ref, weighted)
    respond(weighted, far_ref, turned_ref, weights(energy_ref[...], far_energy_ref[...]), terms_ref)
    finished(stores)


def first_kernel(flag_smem, *refs):
    piece_refs = refs[:4]
    (beside_ref, moved_ref, potential_ref, order_ref, energy_ref, far_energy_ref, other_ref,
     far_out, terms_ref, own_terms, far_ref, weighted_ref, column_ref, sems) = refs[4:]

    @pl.when(flag_smem[0] == 1)
    def _():
        last = piece_refs[3]
        start = GRID - last.shape[0]
        copies = started(sems, (last, far_ref.at[pl.ds(start, last.shape[0])]), first=1)
        start = 0
        for piece in piece_refs[:3]:
            far_ref[start : start + piece.shape[0], :] = piece[...]
            start += piece.shape[0]
        finished(copies)

    @pl.when(flag_smem[0] == 0)
    def _():
        far_ref[...] = beside_ref[...]

    stores = started(sems, (far_ref, far_out))
    weight = weights(energy_ref[...], far_energy_ref[...])
    weigh(potential_ref, moved_ref, weighted_ref)
    mark_columns(order_ref, column_ref)
    respond(weighted_ref, far_ref, moved_ref, weight, own_terms)
    from_far_order(own_terms[...], order_ref, column_ref, terms_ref, 0)
    terms_ref[ROWS:, :] = other_ref[...]
    finished(stores)


def exact_dot(left, right):
    return jnp.dot(left, right, precision=lax.Precision.HIGHEST, preferred_element_type=jnp.float32)


def last_kernel(density_ref, external_ref, even_ref, odd_ref, into_ref, back_ref, screen_ref, even_t_ref, odd_t_ref,
                first_in, second_in, moved_in, turned_in, order_ref,
                energy_ref, first_energy_ref, second_energy_ref,
                response_ref, terms_ref, parts, potential, moved_potential, weighted, own_terms,
                first_ref, second_ref, moved_ref, turned_ref, column_ref, sems):
    loads = started(sems, (moved_in, moved_ref), (first_in, first_ref))
    later = started(sems, (turned_in, turned_ref), (second_in, second_ref), first=2)
    mark_columns(order_ref, column_ref)
    low_half = lax.broadcasted_iota(jnp.int32, (ROWS, LANES), 1) < GY
    along_y = exact_dot(density_ref[...], into_ref[...])
    for q_index in range(NQ):
        at = slice(q_index * ROWS, (q_index + 1) * ROWS)
        spectrum = exact_dot(even_ref[...], along_y[at, :LANES]) + exact_dot(odd_ref[...], along_y[at, LANES:])
        back = exact_dot(spectrum * screen_ref[...], back_ref[...])
        field = jnp.where(low_half, exact_dot(even_t_ref[...], back), exact_dot(odd_t_ref[...], back))
        potential[at, :] = external_ref[...] + field
    moved_potential[...] = to_far_order(potential.at[0:ROWS], order_ref, column_ref, parts)
    finished(loads)
    weigh(moved_potential, moved_ref, weighted)
    weight = weights(energy_ref[...], first_energy_ref[...])
    response_ref[0] = respond(weighted, first_ref, moved_ref, weight, own_terms).T
    from_far_order(own_terms[...], order_ref, column_ref, terms_ref, 0)
    finished(later)
    weigh(potential.at[ROWS : 2 * ROWS], turned_ref, weighted)
    weight = weights(energy_ref[...], second_energy_ref[...])
    response_ref[1] = respond(weighted, second_ref, turned_ref, weight, own_terms).T
    terms_ref[ROWS:, :] = own_terms[...]


def coulomb_tables():
    table = hartley_table(GX)
    other = hartley_table(GY)
    none = np.zeros((GY, 2 * GY))
    twice = np.concatenate([other, other], axis=1)
    into = np.concatenate([np.concatenate([twice, none]), np.concatenate([none, twice])], axis=1)
    back = np.concatenate([twice, none])
    screen = screening(GX, GY)
    screen = np.concatenate([screen, screen], axis=1)
    even, odd = table[:, 0::2], table[:, 1::2]
    return [part.astype(np.float32) for part in (even, odd, into, back, screen, even.T, odd.T)]


VMEM = pl.BlockSpec(memory_space=pltpu.VMEM)
SMEM = pl.BlockSpec(memory_space=pltpu.SMEM)
HBM = pl.BlockSpec(memory_space=pltpu.HBM)
KEPT = pl.BlockSpec(memory_space=pltpu.VMEM)
PLACES = {id(HBM): pltpu.HBM, id(KEPT): pltpu.VMEM}


def local_call(kernel, arrays, in_specs, outs, scratch, copies, microseconds, limit=None):
    return pl.pallas_call(
        kernel,
        out_shape=[
            PLACES.get(id(spec), jax.ShapeDtypeStruct)(shape, kind) for shape, kind, spec in outs
        ],
        in_specs=in_specs,
        out_specs=[spec for shape, kind, spec in outs],
        scratch_shapes=[pltpu.VMEM(shape, kind) for shape, kind in scratch] + [pltpu.SemaphoreType.DMA((copies,))],
        cost_estimate=pl.CostEstimate(flops=0, bytes_accessed=microseconds * 3000000, transcendentals=0),
        compiler_params=pltpu.CompilerParams(vmem_limit_bytes=limit),
    )(*arrays)


F32 = jnp.float32
BF16 = jnp.bfloat16
TALL = (GRID, BANDS)
TURNED = (BANDS, GRID)
BLOCKS = (ROWS, LANES)


def prepare(order, own, order_blocks, external):
    return local_call(
        prepare_kernel, (order, own, order_blocks, external), [SMEM, VMEM, VMEM, VMEM],
        [(TURNED, BF16, KEPT)] * 2 + [(BLOCKS, F32, VMEM)] + [(TURNED, BF16, HBM)] * 2,
        [(TALL, F32), (TALL, F32), ((3 * ROWS, GRID), BF16), (TURNED, BF16)], 2, 10,
        LIMIT,
    )


def second_round_one(order, sent, turned, external, energy, far_energy):
    sent = pltpu.with_memory_space_constraint(sent, pltpu.VMEM)
    turned = pltpu.with_memory_space_constraint(turned, pltpu.VMEM)
    return local_call(
        second_kernel, (order, sent, turned, external, energy, far_energy),
        [SMEM, VMEM, VMEM, VMEM, VMEM, VMEM],
        [(TALL, BF16, HBM), (BLOCKS, F32, VMEM)],
        [(TALL, F32), (TALL, F32), (TURNED, BF16), (TALL, BF16)], 1, 7, LIMIT,
    )


def first_round_one(flag, pieces, beside, moved, potential, order_blocks, energy, far_energy, other):
    places = [pltpu.VMEM] * 3 + [pltpu.HBM]
    pieces = [pltpu.with_memory_space_constraint(piece, place) for piece, place in zip(pieces, places)]
    beside = pltpu.with_memory_space_constraint(beside, pltpu.VMEM)
    moved = pltpu.with_memory_space_constraint(moved, pltpu.VMEM)
    return local_call(
        first_kernel, (flag, *pieces, beside, moved, potential, order_blocks, energy, far_energy, other),
        [SMEM] + [VMEM] * 3 + [HBM] + [VMEM] * 7,
        [(TALL, BF16, HBM), ((2 * ROWS, LANES), F32, VMEM)],
        [(BLOCKS, F32), (TALL, BF16), (TURNED, BF16), (TURNED, BF16)], 2, 3, LIMIT,
    )


def round_two(density, external, first, second, moved, turned, order_blocks, energy, first_energy, second_energy):
    arrays = (density, external, *[jnp.asarray(part) for part in coulomb_tables()], first, second, moved, turned,
              order_blocks, energy, first_energy, second_energy)
    return local_call(
        last_kernel, arrays, [VMEM] * 9 + [HBM] * 4 + [VMEM] * 4,
        [((NQ, BANDS, BANDS), F32, VMEM), ((2 * ROWS, LANES), F32, VMEM)],
        [((3 * ROWS, GRID), BF16), ((2 * ROWS, LANES), F32), (BLOCKS, F32), (TURNED, BF16), (BLOCKS, F32)]
        + [(TALL, BF16)] * 2 + [(TURNED, BF16)] * 3, 4, 5,
    )


def exchange(value, axes):
    return lax.all_to_all(value, axes, 0, 0, tiled=True)


def summed_everywhere(value):
    plane = lax.axis_size(PLANE)
    column = lax.axis_size(COLUMN)
    chunks = value.reshape(plane, -1, LANES)
    part = jnp.sum(exchange(chunks, PLANE), axis=0)
    copies = jnp.broadcast_to(part[None], (column,) + part.shape)
    part = jnp.sum(exchange(copies, COLUMN), axis=0)
    copies = jnp.broadcast_to(part[None], (plane,) + part.shape)
    return exchange(copies, PLANE).reshape(value.shape)


def next_along(value, axis):
    count = lax.axis_size(axis)
    return lax.ppermute(value, axis, [(source, (source - 1) % count) for source in range(count)])


def iterate(states, energies, external, reorder):
    orbital = states[0]
    external = external.reshape(BLOCKS)
    order_blocks = reorder[0, 0].reshape(BLOCKS)
    column_index = lax.axis_index("x")

    cuts = (0, 1248, 1984, 2720, GRID)
    parts = [orbital[cuts[c] : cuts[c + 1]] for c in range(4)]
    count = lax.axis_size("zh")
    hops = [(4 * source, 4 * ((source - 1) % count)) for source in range(count)]
    hop0 = lax.ppermute(parts[0], KX, hops)
    spread = [lax.ppermute(parts[c], "x", [(0, c)]) for c in range(1, 4)]
    far_second = next_along(orbital, KY)
    beside = lax.ppermute(orbital, "x", [(1, 0), (2, 1), (3, 2)])
    inner = jnp.where(column_index == 1, spread[0], spread[1])
    outer, inner, own = lax.optimization_barrier((spread[2], inner, orbital))
    hop3 = lax.ppermute(outer, KX, [(s + 3, t + 3) for s, t in hops])
    hop12 = lax.ppermute(inner, KX, [(s + x, t + x) for s, t in hops for x in (1, 2)])
    second_energy = next_along(energies, KY)
    first_energy = next_along(energies, KX)

    turned, moved, potential, turned_late, moved_late = prepare(reorder[0, 0], own, order_blocks, external)
    potential, hop0, hop12 = lax.optimization_barrier((potential, hop0, hop12))
    pieces = [lax.ppermute(hop0, "x", [(0, 3)])]
    pieces += [lax.ppermute(hop12, "x", [(x, 3)]) for x in (1, 2)]
    second_states, second_terms = second_round_one(reorder[1, 0], far_second, turned, external, energies, second_energy)
    flag = (column_index == 3).astype(jnp.int32).reshape(1)
    first_states, terms = first_round_one(
        flag, pieces + [hop3], beside, moved, potential, order_blocks, energies, first_energy, second_terms
    )
    response, terms = round_two(
        summed_everywhere(terms), external, first_states, second_states, moved_late, turned_late, order_blocks,
        energies, first_energy, second_energy,
    )
    density = summed_everywhere(terms)
    return (response.reshape(1, NQ, 1, BANDS, BANDS), density.reshape(NQ, 1, GRID))


def solution(mesh):
    fine = Mesh(mesh.devices.reshape(AXIS_SIZES), AXES)
    return jax.shard_map(
        iterate,
        mesh=fine,
        in_specs=(
            P(AXES, None, None),
            P(AXES, None),
            P(),
            P(None, AXES, None),
        ),
        out_specs=(P(AXES, None, None, None, None), P()),
        check_vma=False,
    )
```

profile of v0, /device:TPU:1, one launch (start us, length us, event | category | flops | bytes accessed | tf_op | source)
XLA Modules:
  0.0 178.6 jit_solution(4815092569064859069)
XLA Ops:
  0.6 8.9 %collective-permute-start.11 = (bf16[4096,128]{1,0:T(8,128)(2,1)}, bf16[4096,128]{1,0:T(8,128)(2,1)}, u32[]{:S(2)}, u32[]{:S(2)}) collective-permute-start(bf16[4096,128]{1,0:T(8,128)(2,1)} %bitcast.21), channel_id=1, source_target_pairs={{0,31},{1,0},{2,1},{3,2},{4,3},{5,4},{6,5},{7,6},{8,7},{9,8},{10,9... | collective-permute-start | bytes 3145736 | tf_op jit(solution)/shard_map/ppermute | solution.py:367
  9.5 1.3 collective-permute-start.9
  11.9 4.0 %collective-permute-start.1 = (bf16[736,128]{1,0:T(8,128)(2,1)S(1)}, bf16[736,128]{1,0:T(8,128)(2,1)S(1)}, u32[]{:S(2)}, u32[]{:S(2)}) collective-permute-start(bf16[736,128]{1,0:T(8,128)(2,1)S(1)} %get-tuple-element.43), channel_id=1, source_target_pairs={{0,32},{1,33},{2,34},{3,35},{4,36},{5,37},{6,38},{7,39},{8,40},{9,... | collective-permute-start | bytes 565256 | tf_op jit(solution)/shard_map/ppermute | solution.py:381
  15.9 1.3 collective-permute-start.2
  18.2 2.1 %collective-permute-start = (bf16[1376,128]{1,0:T(8,128)(2,1)S(1)}, bf16[1376,128]{1,0:T(8,128)(2,1)}, u32[]{:S(2)}, u32[]{:S(2)}) collective-permute-start(bf16[1376,128]{1,0:T(8,128)(2,1)S(1)} %slice_bitcast_fusion), channel_id=1, source_target_pairs={{0,96},{1,97},{2,98},{3,99},{4,100},{5,101},{6,102},{7,103},{8,104... | collective-permute-start | bytes 1056776 | tf_op jit(solution)/shard_map/ppermute | solution.py:381
  20.3 8.0 %collective-permute-start.3 = (bf16[1248,128]{1,0:T(8,128)(2,1)S(1)}, bf16[1248,128]{1,0:T(8,128)(2,1)}, u32[]{:S(2)}, u32[]{:S(2)}) collective-permute-start(bf16[1248,128]{1,0:T(8,128)(2,1)S(1)} %slice_bitcast_fusion.1), channel_id=1, source_target_pairs={{0,384},{128,0},{256,128},{384,256},{1,385},{129,1},{257,129},{385... | collective-permute-start | bytes 958472 | tf_op jit(solution)/shard_map/ppermute | solution.py:380
  28.4 1.4 collective-permute-start.4
  29.8 1.4 collective-permute-start.8
  31.9 9.5 %shard_map.122 = (bf16[128,4096]{1,0:T(8,128)(2,1)S(1)}, bf16[128,4096]{1,0:T(8,128)(2,1)S(1)}, f32[32,128]{1,0:T(8,128)S(1)}, bf16[128,4096]{1,0:T(8,128)(2,1)}, bf16[128,4096]{1,0:T(8,128)(2,1)}) custom-call(s32[4096]{0:T(1024)S(1)} %bitcast.24, bf16[4096,128]{1,0:T(8,128)(2,1)S(1)} %bitcast.23, s32[32,128]{1,0:T(8,128)S(1)} %bitcast.25, ...), custom_call_target="tpu_custom_call" | custom-call | bytes 30000000 | tf_op jit(solution)/shard_map/pallas_call | solution.py:286
  42.4 12.1 %collective-permute-done.3 = bf16[1248,128]{1,0:T(8,128)(2,1)} collective-permute-done((bf16[1248,128]{1,0:T(8,128)(2,1)S(1)}, bf16[1248,128]{1,0:T(8,128)(2,1)}, u32[]{:S(2)}, u32[]{:S(2)}) %collective-permute-start.3) | collective-permute-done | bytes 319520 | tf_op jit(solution)/shard_map/ppermute | solution.py:380
  54.5 1.3 collective-permute-start.5
  55.8 2.9 %collective-permute-start.12 = (bf16[1,128]{1,0:T(2,128)(2,1)S(1)}, bf16[1,128]{1,0:T(2,128)(2,1)S(1)}, u32[]{:S(2)}, u32[]{:S(2)}) collective-permute-start(bf16[1,128]{1,0:T(2,128)(2,1)S(1)} %copy-done.5), channel_id=1, source_target_pairs={{0,31},{1,0},{2,1},{3,2},{4,3},{5,4},{6,5},{7,6},{8,7},{9,8},{10,9... | collective-permute-start | bytes 776 | tf_op jit(solution)/shard_map/ppermute | solution.py:367
  58.8 2.9 %collective-permute-done.12.far_energy_ref.second_energy_ref = bf16[1,128]{1,0:T(2,128)(2,1)S(1)} collective-permute-done((bf16[1,128]{1,0:T(2,128)(2,1)S(1)}, bf16[1,128]{1,0:T(2,128)(2,1)S(1)}, u32[]{:S(2)}, u32[]{:S(2)}) %collective-permute-start.12) | collective-permute-done | bytes 288 | tf_op jit(solution)/shard_map/ppermute | solution.py:367
  61.7 13.0 %collective-permute-start.10 = (bf16[1,128]{1,0:T(2,128)(2,1)S(1)}, bf16[1,128]{1,0:T(2,128)(2,1)S(1)}, u32[]{:S(2)}, u32[]{:S(2)}) collective-permute-start(bf16[1,128]{1,0:T(2,128)(2,1)S(1)} %copy-done.5), channel_id=1, source_target_pairs={{0,480},{32,0},{64,32},{96,64},{128,96},{160,128},{192,160},{224,1... | collective-permute-start | bytes 776 | tf_op jit(solution)/shard_map/ppermute | solution.py:367
  76.8 1.2 copy-done.2
  78.0 6.6 %shard_map.123 = (bf16[4096,128]{1,0:T(8,128)(2,1)}, f32[32,128]{1,0:T(8,128)S(1)}) custom-call(s32[4096]{0:T(1024)S(1)} %bitcast.31, bf16[4096,128]{1,0:T(8,128)(2,1)} %collective-permute-done.11.sent_ref, bf16[128,4096]{1,0:T(8,128)(2,1)S(1)} %copy-done.2, f32[32,128]{1,0:T(8,128)S(1)} %bitcast.30, bf16[1,128]{1,0:T(2,128)(2,1)S(1)} %copy-done.5, ...), custom_call_target="tpu_custom_call" | custom-call | bytes 21000000 | tf_op jit(solution)/shard_map/pallas_call | solution.py:286
  84.7 1.8 shard_map.124
  86.5 17.3 %all_to_all.30 = f32[32,2,128]{2,1,0:T(2,128)S(1)} all-to-all(f32[32,2,128]{2,1,0:T(2,128)S(1)} %bitcast.32), channel_id=1, replica_groups=mesh['zh'=4,'x'=4,'y'=4,'zl'=4,'core'=2] {'x','y','core'}, dimensions={0} | all-to-all | bytes 65536 | tf_op jit(solution)/shard_map/all_to_all | solution.py:351
  103.8 18.7 %all_to_all.31 = f32[16,2,128]{2,1,0:T(2,128)S(1)} all-to-all(f32[16,2,128]{2,1,0:T(2,128)S(1)} %broadcast_in_dim.8), channel_id=1, replica_groups=mesh['zh'=4,'x'=4,'y'=4,'zl'=4,'core'=2] {'zh','zl'}, dimensions={0} | all-to-all | bytes 32768 | tf_op jit(solution)/shard_map/all_to_all | solution.py:351
  122.5 12.5 %all_to_all.32 = f32[32,2,128]{2,1,0:T(2,128)} all-to-all(f32[32,2,128]{2,1,0:T(2,128)S(1)} %broadcast_in_dim.9), channel_id=1, replica_groups=mesh['zh'=4,'x'=4,'y'=4,'zl'=4,'core'=2] {'x','y','core'}, dimensions={0} | all-to-all | bytes 65536 | tf_op jit(solution)/shard_map/all_to_all | solution.py:351
  135.0 5.8 %shard_map.125 = (f32[2,128,128]{2,1,0:T(8,128)}, f32[64,128]{1,0:T(8,128)}) custom-call(f32[64,128]{1,0:T(8,128)} %bitcast.33, f32[32,128]{1,0:T(8,128)} %bitcast.28, f32[64,32]{1,0:T(8,128)} %constant.26.clone.even_ref, f32[64,32]{1,0:T(8,128)} %constant.27.clone.odd_ref, f32[128,256]{1,0:T(8,128)} %constant.28.clone.into_ref, ...), custom_call_target="tpu_custom_call" | custom-call | bytes 15000000 | tf_op jit(solution)/shard_map/pallas_call | solution.py:286
  140.8 11.3 %all_to_all.33 = f32[32,2,128]{2,1,0:T(2,128)S(1)} all-to-all(f32[32,2,128]{2,1,0:T(2,128)} %bitcast.35), channel_id=1, replica_groups=mesh['zh'=4,'x'=4,'y'=4,'zl'=4,'core'=2] {'x','y','core'}, dimensions={0} | all-to-all | bytes 65536 | tf_op jit(solution)/shard_map/all_to_all | solution.py:351
  152.2 13.9 %all_to_all.34 = f32[16,2,128]{2,1,0:T(2,128)S(1)} all-to-all(f32[16,2,128]{2,1,0:T(2,128)S(1)} %broadcast_in_dim.10), channel_id=1, replica_groups=mesh['zh'=4,'x'=4,'y'=4,'zl'=4,'core'=2] {'zh','zl'}, dimensions={0} | all-to-all | bytes 32768 | tf_op jit(solution)/shard_map/all_to_all | solution.py:351
  166.1 11.9 %all_to_all.35 = f32[32,2,128]{2,1,0:T(2,128)S(1)} all-to-all(f32[32,2,128]{2,1,0:T(2,128)S(1)} %broadcast_in_dim.11), channel_id=1, replica_groups=mesh['zh'=4,'x'=4,'y'=4,'zl'=4,'core'=2] {'x','y','core'}, dimensions={0} | all-to-all | bytes 65536 | tf_op jit(solution)/shard_map/all_to_all | solution.py:351
  (44 shorter events, 6.7 us)
Async XLA Ops:
  0.6 19.6 %copy-start = (bf16[1,4096,128]{2,1,0:T(8,128)(2,1)S(1)}, bf16[1,4096,128]{2,1,0:T(8,128)(2,1)}, u32[]{:S(2)}) copy-start(bf16[1,4096,128]{2,1,0:T(8,128)(2,1)} %param.11) | copy-start | bytes 3145732
  0.6 75.4 %collective-permute-start.11 = (bf16[4096,128]{1,0:T(8,128)(2,1)}, bf16[4096,128]{1,0:T(8,128)(2,1)}, u32[]{:S(2)}, u32[]{:S(2)}) collective-permute-start(bf16[4096,128]{1,0:T(8,128)(2,1)} %bitcast.21), channel_id=1, source_target_pairs={{0,31},{1,0},{2,1},{3,2},{4,3},{5,4},{6,5},{7,6},{8,7},{9,8},{10,9... | collective-permute-start | bytes 3145736 | tf_op jit(solution)/shard_map/ppermute | solution.py:367
  9.5 75.1 %collective-permute-start.9 = (bf16[4096,128]{1,0:T(8,128)(2,1)}, bf16[4096,128]{1,0:T(8,128)(2,1)S(1)}, u32[]{:S(2)}, u32[]{:S(2)}) collective-permute-start(bf16[4096,128]{1,0:T(8,128)(2,1)} %bitcast.22), channel_id=1, source_target_pairs={{32,0},{64,32},{96,64},{33,1},{65,33},{97,65},{34,2},{66,34},{98,6... | collective-permute-start | bytes 3145736 | tf_op jit(solution)/shard_map/ppermute | solution.py:383
  11.9 8.4 %collective-permute-start.1 = (bf16[736,128]{1,0:T(8,128)(2,1)S(1)}, bf16[736,128]{1,0:T(8,128)(2,1)S(1)}, u32[]{:S(2)}, u32[]{:S(2)}) collective-permute-start(bf16[736,128]{1,0:T(8,128)(2,1)S(1)} %get-tuple-element.43), channel_id=1, source_target_pairs={{0,32},{1,33},{2,34},{3,35},{4,36},{5,37},{6,38},{7,39},{8,40},{9,... | collective-permute-start | bytes 565256 | tf_op jit(solution)/shard_map/ppermute | solution.py:381
  15.9 12.5 %collective-permute-start.2 = (bf16[736,128]{1,0:T(8,128)(2,1)S(1)}, bf16[736,128]{1,0:T(8,128)(2,1)S(1)}, u32[]{:S(2)}, u32[]{:S(2)}) collective-permute-start(bf16[736,128]{1,0:T(8,128)(2,1)S(1)} %get-tuple-element.42), channel_id=1, source_target_pairs={{0,64},{1,65},{2,66},{3,67},{4,68},{5,69},{6,70},{7,71},{8,72},{9,... | collective-permute-start | bytes 565256 | tf_op jit(solution)/shard_map/ppermute | solution.py:381
  18.2 10.2 %collective-permute-start = (bf16[1376,128]{1,0:T(8,128)(2,1)S(1)}, bf16[1376,128]{1,0:T(8,128)(2,1)}, u32[]{:S(2)}, u32[]{:S(2)}) collective-permute-start(bf16[1376,128]{1,0:T(8,128)(2,1)S(1)} %slice_bitcast_fusion), channel_id=1, source_target_pairs={{0,96},{1,97},{2,98},{3,99},{4,100},{5,101},{6,102},{7,103},{8,104... | collective-permute-start | bytes 1056776 | tf_op jit(solution)/shard_map/ppermute | solution.py:381
  20.3 10.9 %copy-start.8 = (s32[2,1,4096]{2,1,0:T(1,128)S(1)}, s32[2,1,4096]{2,1,0:T(1,128)}, u32[]{:S(2)}) copy-start(s32[2,1,4096]{2,1,0:T(1,128)} %param.14) | copy-start | bytes 98308
  20.3 34.2 %collective-permute-start.3 = (bf16[1248,128]{1,0:T(8,128)(2,1)S(1)}, bf16[1248,128]{1,0:T(8,128)(2,1)}, u32[]{:S(2)}, u32[]{:S(2)}) collective-permute-start(bf16[1248,128]{1,0:T(8,128)(2,1)S(1)} %slice_bitcast_fusion.1), channel_id=1, source_target_pairs={{0,384},{128,0},{256,128},{384,256},{1,385},{129,1},{257,129},{385... | collective-permute-start | bytes 958472 | tf_op jit(solution)/shard_map/ppermute | solution.py:380
  28.4 26.1 %collective-permute-start.4 = (bf16[736,128]{1,0:T(8,128)(2,1)S(1)}, bf16[736,128]{1,0:T(8,128)(2,1)}, u32[]{:S(2)}, u32[]{:S(2)}) collective-permute-start(bf16[736,128]{1,0:T(8,128)(2,1)S(1)} %broadcast_select_fusion), channel_id=1, source_target_pairs={{32,416},{64,448},{160,32},{192,64},{288,160},{320,192},{416,288},... | collective-permute-start | bytes 565256 | tf_op jit(solution)/shard_map/ppermute | solution.py:387
  29.8 54.9 %collective-permute-start.8 = (bf16[1376,128]{1,0:T(8,128)(2,1)}, bf16[1376,128]{1,0:T(8,128)(2,1)}, u32[]{:S(2)}, u32[]{:S(2)}) collective-permute-start(bf16[1376,128]{1,0:T(8,128)(2,1)} %collective-permute-done), channel_id=1, source_target_pairs={{96,480},{224,96},{352,224},{480,352},{97,481},{225,97},{353,225},... | collective-permute-start | bytes 1056776 | tf_op jit(solution)/shard_map/ppermute | solution.py:386
  31.2 0.7 copy-start.4
  31.2 53.5 %copy-start.3 = (s32[1,1,4096]{2,1,0:T(1,128)}, s32[1,1,4096]{2,1,0:T(1,128)S(1)}, u32[]{:S(2)}) copy-start(s32[1,1,4096]{2,1,0:T(1,128)S(1)} %get-tuple-element.45) | copy-start | bytes 49156
  41.4 1.0 copy-start.1
  42.4 13.5 %copy-start.5 = (bf16[1,128]{1,0:T(2,128)(2,1)S(1)}, bf16[1,128]{1,0:T(2,128)(2,1)}, u32[]{:S(2)}) copy-start(bf16[1,128]{1,0:T(2,128)(2,1)} %energy_ref.3) | copy-start | bytes 772
  54.5 30.1 %collective-permute-start.5 = (bf16[1248,128]{1,0:T(8,128)(2,1)}, bf16[1248,128]{1,0:T(8,128)(2,1)S(1)}, u32[]{:S(2)}, u32[]{:S(2)}) collective-permute-start(bf16[1248,128]{1,0:T(8,128)(2,1)} %collective-permute-done.3), channel_id=1, source_target_pairs={{0,96},{1,97},{2,98},{3,99},{4,100},{5,101},{6,102},{7,103},{8,104... | collective-permute-start | bytes 958472 | tf_op jit(solution)/shard_map/ppermute | solution.py:393
  55.8 5.8 %collective-permute-start.12 = (bf16[1,128]{1,0:T(2,128)(2,1)S(1)}, bf16[1,128]{1,0:T(2,128)(2,1)S(1)}, u32[]{:S(2)}, u32[]{:S(2)}) collective-permute-start(bf16[1,128]{1,0:T(2,128)(2,1)S(1)} %copy-done.5), channel_id=1, source_target_pairs={{0,31},{1,0},{2,1},{3,2},{4,3},{5,4},{6,5},{7,6},{8,7},{9,8},{10,9... | collective-permute-start | bytes 776 | tf_op jit(solution)/shard_map/ppermute | solution.py:367
  61.7 15.1 %copy-start.7 = (bf16[1,128]{1,0:T(2,128)(2,1)}, bf16[1,128]{1,0:T(2,128)(2,1)S(1)}, u32[]{:S(2)}) copy-start(bf16[1,128]{1,0:T(2,128)(2,1)S(1)} %collective-permute-done.12.far_energy_ref.second_energy_ref) | copy-start | bytes 772
  61.7 13.7 %collective-permute-start.10 = (bf16[1,128]{1,0:T(2,128)(2,1)S(1)}, bf16[1,128]{1,0:T(2,128)(2,1)S(1)}, u32[]{:S(2)}, u32[]{:S(2)}) collective-permute-start(bf16[1,128]{1,0:T(2,128)(2,1)S(1)} %copy-done.5), channel_id=1, source_target_pairs={{0,480},{32,0},{64,32},{96,64},{128,96},{160,128},{192,160},{224,1... | collective-permute-start | bytes 776 | tf_op jit(solution)/shard_map/ppermute | solution.py:367
  75.4 9.3 %copy-start.6 = (bf16[1,128]{1,0:T(2,128)(2,1)}, bf16[1,128]{1,0:T(2,128)(2,1)S(1)}, u32[]{:S(2)}) copy-start(bf16[1,128]{1,0:T(2,128)(2,1)S(1)} %collective-permute-done.10.refs_9_.first_energy_ref) | copy-start | bytes 772
  75.4 9.3 %collective-permute-start.6 = (bf16[736,128]{1,0:T(8,128)(2,1)}, bf16[736,128]{1,0:T(8,128)(2,1)S(1)}, u32[]{:S(2)}, u32[]{:S(2)}) collective-permute-start(bf16[736,128]{1,0:T(8,128)(2,1)} %collective-permute-done.4), channel_id=1, source_target_pairs={{32,96},{33,97},{34,98},{35,99},{36,100},{37,101},{38,102},{39,103... | collective-permute-start | bytes 565256 | tf_op jit(solution)/shard_map/ppermute | solution.py:394
  76.1 8.6 %collective-permute-start.7 = (bf16[736,128]{1,0:T(8,128)(2,1)}, bf16[736,128]{1,0:T(8,128)(2,1)S(1)}, u32[]{:S(2)}, u32[]{:S(2)}) collective-permute-start(bf16[736,128]{1,0:T(8,128)(2,1)} %collective-permute-done.4), channel_id=1, source_target_pairs={{64,96},{65,97},{66,98},{67,99},{68,100},{69,101},{70,102},{71,103... | collective-permute-start | bytes 565256 | tf_op jit(solution)/shard_map/ppermute | solution.py:394
  76.8 1.2 copy-start.2
where the time goes:
time: 179 us
  blocking collectives  85.5 us (48%)
  starting transfers between devices  46.9 us (26%)
  Pallas kernels  23.6 us (13%)
  waiting for transfers between devices  15.7 us (9%)
  local copies, waits for them, and re-layouts  5.7 us (3%)
    all_to_all x6, blocking collectives, exchange(): return lax.all_to_all(value, axes, 0, 0, tiled=True)  85.5 us
    ppermute x3, starting transfers between devices, next_along(): lax.ppermute(value, axis, [(source, (source - 1) % count) for source in r...  24.8 us
    pallas_call x4, Pallas kernels, local_call(): pl.pallas_call(kernel, out_shape=[PLACES.get(id(spec), jax.ShapeDtypeStru...  23.6 us
    ppermute x1, waiting for transfers between devices, iterate(): hop0 = lax.ppermute(parts[0], KX, hops)  12.1 us
    ppermute x1, starting transfers between devices, iterate(): hop0 = lax.ppermute(parts[0], KX, hops)  8.02 us
    ppermute x3, starting transfers between devices, iterate(): spread = [lax.ppermute(parts[c], 'x', [(0, c)]) for c in range(1, 4)]  7.36 us
    unnamed x19, local copies, waits for them, and re-layouts  3.58 us
  transfers between devices with their start and end apart: 13, of which 3 were waited for; matrix products, arithmetic and copies ran while one was open for 1% of the time, Pallas kernels for 9%

commit v1 on v0

--- a/solution.py
+++ b/solution.py
@@ -373,7 +373,7 @@
     order_blocks = reorder[0, 0].reshape(BLOCKS)
     column_index = lax.axis_index("x")
 
-    cuts = (0, 1248, 1984, 2720, GRID)
+    cuts = (0, 1152, 1856, 2560, GRID)
     parts = [orbital[cuts[c] : cuts[c + 1]] for c in range(4)]
     count = lax.axis_size("zh")
     hops = [(4 * source, 4 * ((source - 1) % count)) for source in range(count)]
@@ -382,17 +382,16 @@
     far_second = next_along(orbital, KY)
     beside = lax.ppermute(orbital, "x", [(1, 0), (2, 1), (3, 2)])
     inner = jnp.where(column_index == 1, spread[0], spread[1])
-    outer, inner, own = lax.optimization_barrier((spread[2], inner, orbital))
-    hop3 = lax.ppermute(outer, KX, [(s + 3, t + 3) for s, t in hops])
+    hop3 = lax.ppermute(spread[2], KX, [(s + 3, t + 3) for s, t in hops])
     hop12 = lax.ppermute(inner, KX, [(s + x, t + x) for s, t in hops for x in (1, 2)])
     second_energy = next_along(energies, KY)
     first_energy = next_along(energies, KX)
 
-    turned, moved, potential, turned_late, moved_late = prepare(reorder[0, 0], own, order_blocks, external)
-    potential, hop0, hop12 = lax.optimization_barrier((potential, hop0, hop12))
+    turned, moved, potential, turned_late, moved_late = prepare(reorder[0, 0], orbital, order_blocks, external)
+    second_states, second_terms = second_round_one(reorder[1, 0], far_second, turned, external, energies, second_energy)
+    second_terms, hop0, hop12 = lax.optimization_barrier((second_terms, hop0, hop12))
     pieces = [lax.ppermute(hop0, "x", [(0, 3)])]
     pieces += [lax.ppermute(hop12, "x", [(x, 3)]) for x in (1, 2)]
-    second_states, second_terms = second_round_one(reorder[1, 0], far_second, turned, external, energies, second_energy)
     flag = (column_index == 3).astype(jnp.int32).reshape(1)
     first_states, terms = first_round_one(
         flag, pieces + [hop3], beside, moved, potential, order_blocks, energies, first_energy, second_terms

time: 179 us -> 169 us (0.944)
  waiting for transfers between devices: 15.7 us -> 2.71 us
  blocking collectives: 85.5 us -> 97.3 us
  starting transfers between devices: 46.9 us -> 39.1 us
    all_to_all x6, blocking collectives: 85.5 us -> 97.3 us  [exchange(): return lax.all_to_all(value, axes, 0, 0, tiled=True)]
    ppermute x1, waiting for transfers between devices: 12.1 us -> 0.98 us  [iterate(): hop0 = lax.ppermute(parts[0], KX, hops)]
    ppermute x3, starting transfers between devices: 24.8 us -> 15.3 us  [next_along(): lax.ppermute(value, axis, [(source, (source - 1) % count) for source in r...]
    ppermute x3, waiting for transfers between devices: 3.57 us -> 1.71 us  [next_along(): lax.ppermute(value, axis, [(source, (source - 1) % count) for source in r...]
    unnamed x19 -> x15, local copies, waits for them, and re-layouts: 3.58 us -> 1.98 us
  transfers between devices with their start and end apart: 13 -> 13, of which waited for: 3 -> 2; matrix products, arithmetic and copies ran while one was open for 1% -> 2% of each run, Pallas kernels for 9% -> 10%
where the time goes in v1:
time: 169 us
  blocking collectives  97.3 us (58%)
  starting transfers between devices  39.1 us (23%)
  Pallas kernels  23.6 us (14%)
  local copies, waits for them, and re-layouts  4.78 us (3%)
  waiting for transfers between devices  2.71 us (2%)
    all_to_all x6, blocking collectives, exchange(): return lax.all_to_all(value, axes, 0, 0, tiled=True)  97.3 us
    pallas_call x4, Pallas kernels, local_call(): pl.pallas_call(kernel, out_shape=[PLACES.get(id(spec), jax.ShapeDtypeStru...  23.6 us
    ppermute x3, starting transfers between devices, next_along(): lax.ppermute(value, axis, [(source, (source - 1) % count) for source in r...  15.3 us
    ppermute x1, starting transfers between devices, iterate(): hop0 = lax.ppermute(parts[0], KX, hops)  9.76 us
    ppermute x3, starting transfers between devices, iterate(): spread = [lax.ppermute(parts[c], 'x', [(0, c)]) for c in range(1, 4)]  7.35 us
  transfers between devices with their start and end apart: 13, of which 2 were waited for; matrix products, arithmetic and copies ran while one was open for 2% of the time, Pallas kernels for 10%

profile of v1, /device:TPU:1, one launch (start us, length us, event | category | flops | bytes accessed | tf_op | source)
XLA Modules:
  0.0 168.6 jit_solution(14148145300824823883)
XLA Ops:
  0.6 8.9 %collective-permute-start = (bf16[4096,128]{1,0:T(8,128)(2,1)}, bf16[4096,128]{1,0:T(8,128)(2,1)}, u32[]{:S(2)}, u32[]{:S(2)}) collective-permute-start(bf16[4096,128]{1,0:T(8,128)(2,1)} %bitcast.21), channel_id=1, source_target_pairs={{0,31},{1,0},{2,1},{3,2},{4,3},{5,4},{6,5},{7,6},{8,7},{9,8},{10,9... | collective-permute-start | bytes 3145736 | tf_op jit(solution)/shard_map/ppermute | solution.py:367
  9.5 1.3 collective-permute-start.11
  10.8 1.7 %slice_bitcast_fusion.2 = (bf16[704,128]{1,0:T(8,128)(2,1)S(1)}, bf16[704,128]{1,0:T(8,128)(2,1)}) fusion(bf16[1,4096,128]{2,1,0:T(8,128)(2,1)} %param.11), kind=kLoop, calls=%fused_computation.2 | loop fusion | bytes 720896 | tf_op jit(solution)/shard_map/slice | solution.py:377
  12.5 4.0 %collective-permute-start.3 = (bf16[704,128]{1,0:T(8,128)(2,1)}, bf16[704,128]{1,0:T(8,128)(2,1)S(1)}, u32[]{:S(2)}, u32[]{:S(2)}) collective-permute-start(bf16[704,128]{1,0:T(8,128)(2,1)} %get-tuple-element.37), channel_id=1, source_target_pairs={{0,32},{1,33},{2,34},{3,35},{4,36},{5,37},{6,38},{7,39},{8,40},{9,... | collective-permute-start | bytes 540680 | tf_op jit(solution)/shard_map/ppermute | solution.py:381
  16.5 1.3 collective-permute-start.4
  17.8 1.0 slice_bitcast_fusion
  18.9 2.1 %collective-permute-start.9 = (bf16[1536,128]{1,0:T(8,128)(2,1)S(1)}, bf16[1536,128]{1,0:T(8,128)(2,1)}, u32[]{:S(2)}, u32[]{:S(2)}) collective-permute-start(bf16[1536,128]{1,0:T(8,128)(2,1)S(1)} %slice_bitcast_fusion), channel_id=1, source_target_pairs={{0,96},{1,97},{2,98},{3,99},{4,100},{5,101},{6,102},{7,103},{8,104... | collective-permute-start | bytes 1179656 | tf_op jit(solution)/shard_map/ppermute | solution.py:381
  21.6 4.5 %collective-permute-start.1 = (bf16[1,128]{1,0:T(2,128)(2,1)S(1)}, bf16[1,128]{1,0:T(2,128)(2,1)S(1)}, u32[]{:S(2)}, u32[]{:S(2)}) collective-permute-start(bf16[1,128]{1,0:T(2,128)(2,1)S(1)} %copy-done.3), channel_id=1, source_target_pairs={{0,31},{1,0},{2,1},{3,2},{4,3},{5,4},{6,5},{7,6},{8,7},{9,8},{10,9... | collective-permute-start | bytes 776 | tf_op jit(solution)/shard_map/ppermute | solution.py:367
  26.2 9.8 %collective-permute-start.2 = (bf16[1152,128]{1,0:T(8,128)(2,1)S(1)}, bf16[1152,128]{1,0:T(8,128)(2,1)}, u32[]{:S(2)}, u32[]{:S(2)}) collective-permute-start(bf16[1152,128]{1,0:T(8,128)(2,1)S(1)} %slice_bitcast_fusion.1), channel_id=1, source_target_pairs={{0,384},{128,0},{256,128},{384,256},{1,385},{129,1},{257,129},{385... | collective-permute-start | bytes 884744 | tf_op jit(solution)/shard_map/ppermute | solution.py:380
  36.0 1.4 collective-permute-start.5
  37.4 1.4 collective-permute-start.10
  39.5 9.5 %shard_map.122 = (bf16[128,4096]{1,0:T(8,128)(2,1)S(1)}, bf16[128,4096]{1,0:T(8,128)(2,1)S(1)}, f32[32,128]{1,0:T(8,128)S(1)}, bf16[128,4096]{1,0:T(8,128)(2,1)}, bf16[128,4096]{1,0:T(8,128)(2,1)}) custom-call(s32[4096]{0:T(1024)S(1)} %bitcast.24, bf16[4096,128]{1,0:T(8,128)(2,1)S(1)} %bitcast.23, s32[32,128]{1,0:T(8,128)S(1)} %bitcast.25, ...), custom_call_target="tpu_custom_call" | custom-call | bytes 30000000 | tf_op jit(solution)/shard_map/pallas_call | solution.py:286
  49.0 6.6 %shard_map.123 = (bf16[4096,128]{1,0:T(8,128)(2,1)}, f32[32,128]{1,0:T(8,128)S(1)}) custom-call(s32[4096]{0:T(1024)S(1)} %bitcast.31, bf16[4096,128]{1,0:T(8,128)(2,1)} %collective-permute-done.sent_ref, bf16[128,4096]{1,0:T(8,128)(2,1)S(1)} %get-tuple-element.16.turned_ref, f32[32,128]{1,0:T(8,128)S(1)} %bitcast.30, bf16[1,128]{1,0:T(2,128)(2,1)S(1)} %copy-done.3, ...), custom_call_target="tpu_custom_call" | custom-call | bytes 21000000 | tf_op jit(solution)/shard_map/pallas_call | solution.py:286
  56.6 1.3 collective-permute-start.6
  57.9 1.9 %collective-permute-start.12 = (bf16[1,128]{1,0:T(2,128)(2,1)S(1)}, bf16[1,128]{1,0:T(2,128)(2,1)S(1)}, u32[]{:S(2)}, u32[]{:S(2)}) collective-permute-start(bf16[1,128]{1,0:T(2,128)(2,1)S(1)} %copy-done.3), channel_id=1, source_target_pairs={{0,480},{32,0},{64,32},{96,64},{128,96},{160,128},{192,160},{224,1... | collective-permute-start | bytes 776 | tf_op jit(solution)/shard_map/ppermute | solution.py:367
  60.5 1.7 %collective-permute-done.12.refs_9_.first_energy_ref = bf16[1,128]{1,0:T(2,128)(2,1)S(1)} collective-permute-done((bf16[1,128]{1,0:T(2,128)(2,1)S(1)}, bf16[1,128]{1,0:T(2,128)(2,1)S(1)}, u32[]{:S(2)}, u32[]{:S(2)}) %collective-permute-start.12) | collective-permute-done | bytes 288 | tf_op jit(solution)/shard_map/ppermute | solution.py:367
  62.9 1.7 %shard_map.124 = (bf16[4096,128]{1,0:T(8,128)(2,1)}, f32[64,128]{1,0:T(8,128)S(1)}) custom-call(s32[1]{0:T(128)} %bitcast.flag_smem, bf16[1152,128]{1,0:T(8,128)(2,1)S(1)} %collective-permute-done.6.refs_0_, bf16[704,128]{1,0:T(8,128)(2,1)S(1)} %collective-permute-done.7.refs_1_, bf16[704,128]{1,0:T(8,128)(2,1)S(1)} %collective-permute-done.8.refs_2_, ...), custom_call_target="tpu_custom_call" | custom-call | bytes 9000000 | tf_op jit(solution)/shard_map/pallas_call | solution.py:286
  64.7 27.9 %all_to_all.30 = f32[32,2,128]{2,1,0:T(2,128)S(1)} all-to-all(f32[32,2,128]{2,1,0:T(2,128)S(1)} %bitcast.32), channel_id=1, replica_groups=mesh['zh'=4,'x'=4,'y'=4,'zl'=4,'core'=2] {'x','y','core'}, dimensions={0} | all-to-all | bytes 65536 | tf_op jit(solution)/shard_map/all_to_all | solution.py:351
  92.7 19.8 %all_to_all.31 = f32[16,2,128]{2,1,0:T(2,128)S(1)} all-to-all(f32[16,2,128]{2,1,0:T(2,128)S(1)} %broadcast_in_dim.8), channel_id=1, replica_groups=mesh['zh'=4,'x'=4,'y'=4,'zl'=4,'core'=2] {'zh','zl'}, dimensions={0} | all-to-all | bytes 32768 | tf_op jit(solution)/shard_map/all_to_all | solution.py:351
  112.5 12.4 %all_to_all.32 = f32[32,2,128]{2,1,0:T(2,128)} all-to-all(f32[32,2,128]{2,1,0:T(2,128)S(1)} %broadcast_in_dim.9), channel_id=1, replica_groups=mesh['zh'=4,'x'=4,'y'=4,'zl'=4,'core'=2] {'x','y','core'}, dimensions={0} | all-to-all | bytes 65536 | tf_op jit(solution)/shard_map/all_to_all | solution.py:351
  125.0 5.8 %shard_map.125 = (f32[2,128,128]{2,1,0:T(8,128)}, f32[64,128]{1,0:T(8,128)}) custom-call(f32[64,128]{1,0:T(8,128)} %bitcast.33, f32[32,128]{1,0:T(8,128)} %bitcast.28, f32[64,32]{1,0:T(8,128)} %constant.26.clone.even_ref, f32[64,32]{1,0:T(8,128)} %constant.27.clone.odd_ref, f32[128,256]{1,0:T(8,128)} %constant.28.clone.into_ref, ...), custom_call_target="tpu_custom_call" | custom-call | bytes 15000000 | tf_op jit(solution)/shard_map/pallas_call | solution.py:286
  130.8 11.3 %all_to_all.33 = f32[32,2,128]{2,1,0:T(2,128)S(1)} all-to-all(f32[32,2,128]{2,1,0:T(2,128)} %bitcast.35), channel_id=1, replica_groups=mesh['zh'=4,'x'=4,'y'=4,'zl'=4,'core'=2] {'x','y','core'}, dimensions={0} | all-to-all | bytes 65536 | tf_op jit(solution)/shard_map/all_to_all | solution.py:351
  142.1 13.9 %all_to_all.34 = f32[16,2,128]{2,1,0:T(2,128)S(1)} all-to-all(f32[16,2,128]{2,1,0:T(2,128)S(1)} %broadcast_in_dim.10), channel_id=1, replica_groups=mesh['zh'=4,'x'=4,'y'=4,'zl'=4,'core'=2] {'zh','zl'}, dimensions={0} | all-to-all | bytes 32768 | tf_op jit(solution)/shard_map/all_to_all | solution.py:351
  156.0 11.9 %all_to_all.35 = f32[32,2,128]{2,1,0:T(2,128)S(1)} all-to-all(f32[32,2,128]{2,1,0:T(2,128)S(1)} %broadcast_in_dim.11), channel_id=1, replica_groups=mesh['zh'=4,'x'=4,'y'=4,'zl'=4,'core'=2] {'x','y','core'}, dimensions={0} | all-to-all | bytes 65536 | tf_op jit(solution)/shard_map/all_to_all | solution.py:351
  (40 shorter events, 4.5 us)
Async XLA Ops:
  0.6 20.3 %copy-start = (bf16[1,4096,128]{2,1,0:T(8,128)(2,1)S(1)}, bf16[1,4096,128]{2,1,0:T(8,128)(2,1)}, u32[]{:S(2)}) copy-start(bf16[1,4096,128]{2,1,0:T(8,128)(2,1)} %param.11) | copy-start | bytes 3145732
  0.6 48.3 %collective-permute-start = (bf16[4096,128]{1,0:T(8,128)(2,1)}, bf16[4096,128]{1,0:T(8,128)(2,1)}, u32[]{:S(2)}, u32[]{:S(2)}) collective-permute-start(bf16[4096,128]{1,0:T(8,128)(2,1)} %bitcast.21), channel_id=1, source_target_pairs={{0,31},{1,0},{2,1},{3,2},{4,3},{5,4},{6,5},{7,6},{8,7},{9,8},{10,9... | collective-permute-start | bytes 3145736 | tf_op jit(solution)/shard_map/ppermute | solution.py:367
  9.5 53.4 %collective-permute-start.11 = (bf16[4096,128]{1,0:T(8,128)(2,1)}, bf16[4096,128]{1,0:T(8,128)(2,1)S(1)}, u32[]{:S(2)}, u32[]{:S(2)}) collective-permute-start(bf16[4096,128]{1,0:T(8,128)(2,1)} %bitcast.22), channel_id=1, source_target_pairs={{32,0},{64,32},{96,64},{33,1},{65,33},{97,65},{34,2},{66,34},{98,6... | collective-permute-start | bytes 3145736 | tf_op jit(solution)/shard_map/ppermute | solution.py:383
  12.5 8.5 %collective-permute-start.3 = (bf16[704,128]{1,0:T(8,128)(2,1)}, bf16[704,128]{1,0:T(8,128)(2,1)S(1)}, u32[]{:S(2)}, u32[]{:S(2)}) collective-permute-start(bf16[704,128]{1,0:T(8,128)(2,1)} %get-tuple-element.37), channel_id=1, source_target_pairs={{0,32},{1,33},{2,34},{3,35},{4,36},{5,37},{6,38},{7,39},{8,40},{9,... | collective-permute-start | bytes 540680 | tf_op jit(solution)/shard_map/ppermute | solution.py:381
  16.5 9.6 %collective-permute-start.4 = (bf16[704,128]{1,0:T(8,128)(2,1)S(1)}, bf16[704,128]{1,0:T(8,128)(2,1)S(1)}, u32[]{:S(2)}, u32[]{:S(2)}) collective-permute-start(bf16[704,128]{1,0:T(8,128)(2,1)S(1)} %get-tuple-element.36), channel_id=1, source_target_pairs={{0,64},{1,65},{2,66},{3,67},{4,68},{5,69},{6,70},{7,71},{8,72},{9,... | collective-permute-start | bytes 540680 | tf_op jit(solution)/shard_map/ppermute | solution.py:381
  18.9 18.5 %collective-permute-start.9 = (bf16[1536,128]{1,0:T(8,128)(2,1)S(1)}, bf16[1536,128]{1,0:T(8,128)(2,1)}, u32[]{:S(2)}, u32[]{:S(2)}) collective-permute-start(bf16[1536,128]{1,0:T(8,128)(2,1)S(1)} %slice_bitcast_fusion), channel_id=1, source_target_pairs={{0,96},{1,97},{2,98},{3,99},{4,100},{5,101},{6,102},{7,103},{8,104... | collective-permute-start | bytes 1179656 | tf_op jit(solution)/shard_map/ppermute | solution.py:381
  21.0 0.7 copy-start.3
  21.0 17.8 %copy-start.6 = (s32[2,1,4096]{2,1,0:T(1,128)S(1)}, s32[2,1,4096]{2,1,0:T(1,128)}, u32[]{:S(2)}) copy-start(s32[2,1,4096]{2,1,0:T(1,128)} %param.14) | copy-start | bytes 98308
  21.6 14.3 %collective-permute-start.1 = (bf16[1,128]{1,0:T(2,128)(2,1)S(1)}, bf16[1,128]{1,0:T(2,128)(2,1)S(1)}, u32[]{:S(2)}, u32[]{:S(2)}) collective-permute-start(bf16[1,128]{1,0:T(2,128)(2,1)S(1)} %copy-done.3), channel_id=1, source_target_pairs={{0,31},{1,0},{2,1},{3,2},{4,3},{5,4},{6,5},{7,6},{8,7},{9,8},{10,9... | collective-permute-start | bytes 776 | tf_op jit(solution)/shard_map/ppermute | solution.py:367
  26.2 30.4 %collective-permute-start.2 = (bf16[1152,128]{1,0:T(8,128)(2,1)S(1)}, bf16[1152,128]{1,0:T(8,128)(2,1)}, u32[]{:S(2)}, u32[]{:S(2)}) collective-permute-start(bf16[1152,128]{1,0:T(8,128)(2,1)S(1)} %slice_bitcast_fusion.1), channel_id=1, source_target_pairs={{0,384},{128,0},{256,128},{384,256},{1,385},{129,1},{257,129},{385... | collective-permute-start | bytes 884744 | tf_op jit(solution)/shard_map/ppermute | solution.py:380
  36.0 13.0 %copy-start.5 = (bf16[1,128]{1,0:T(2,128)(2,1)}, bf16[1,128]{1,0:T(2,128)(2,1)S(1)}, u32[]{:S(2)}) copy-start(bf16[1,128]{1,0:T(2,128)(2,1)S(1)} %collective-permute-done.1.far_energy_ref.second_energy_ref) | copy-start | bytes 772
  36.0 20.6 %collective-permute-start.5 = (bf16[704,128]{1,0:T(8,128)(2,1)S(1)}, bf16[704,128]{1,0:T(8,128)(2,1)}, u32[]{:S(2)}, u32[]{:S(2)}) collective-permute-start(bf16[704,128]{1,0:T(8,128)(2,1)S(1)} %broadcast_select_fusion), channel_id=1, source_target_pairs={{32,416},{64,448},{160,32},{192,64},{288,160},{320,192},{416,288},... | collective-permute-start | bytes 540680 | tf_op jit(solution)/shard_map/ppermute | solution.py:386
  37.4 25.5 %collective-permute-start.10 = (bf16[1536,128]{1,0:T(8,128)(2,1)}, bf16[1536,128]{1,0:T(8,128)(2,1)}, u32[]{:S(2)}, u32[]{:S(2)}) collective-permute-start(bf16[1536,128]{1,0:T(8,128)(2,1)} %collective-permute-done.9), channel_id=1, source_target_pairs={{96,480},{224,96},{352,224},{480,352},{97,481},{225,97},{353,225},... | collective-permute-start | bytes 1179656 | tf_op jit(solution)/shard_map/ppermute | solution.py:385
  38.8 0.7 copy-start.2
  38.8 24.1 %copy-start.1 = (s32[1,1,4096]{2,1,0:T(1,128)}, s32[1,1,4096]{2,1,0:T(1,128)S(1)}, u32[]{:S(2)}) copy-start(s32[1,1,4096]{2,1,0:T(1,128)S(1)} %get-tuple-element.38) | copy-start | bytes 49156
  56.6 6.3 %collective-permute-start.6 = (bf16[1152,128]{1,0:T(8,128)(2,1)}, bf16[1152,128]{1,0:T(8,128)(2,1)S(1)}, u32[]{:S(2)}, u32[]{:S(2)}) collective-permute-start(bf16[1152,128]{1,0:T(8,128)(2,1)} %collective-permute-done.2), channel_id=1, source_target_pairs={{0,96},{1,97},{2,98},{3,99},{4,100},{5,101},{6,102},{7,103},{8,104... | collective-permute-start | bytes 884744 | tf_op jit(solution)/shard_map/ppermute | solution.py:393
  57.9 4.3 %collective-permute-start.12 = (bf16[1,128]{1,0:T(2,128)(2,1)S(1)}, bf16[1,128]{1,0:T(2,128)(2,1)S(1)}, u32[]{:S(2)}, u32[]{:S(2)}) collective-permute-start(bf16[1,128]{1,0:T(2,128)(2,1)S(1)} %copy-done.3), channel_id=1, source_target_pairs={{0,480},{32,0},{64,32},{96,64},{128,96},{160,128},{192,160},{224,1... | collective-permute-start | bytes 776 | tf_op jit(solution)/shard_map/ppermute | solution.py:367
  59.8 3.1 %collective-permute-start.7 = (bf16[704,128]{1,0:T(8,128)(2,1)}, bf16[704,128]{1,0:T(8,128)(2,1)S(1)}, u32[]{:S(2)}, u32[]{:S(2)}) collective-permute-start(bf16[704,128]{1,0:T(8,128)(2,1)} %collective-permute-done.5), channel_id=1, source_target_pairs={{32,96},{33,97},{34,98},{35,99},{36,100},{37,101},{38,102},{39,103... | collective-permute-start | bytes 540680 | tf_op jit(solution)/shard_map/ppermute | solution.py:394
  62.2 0.7 copy-start.4
  62.2 0.7 collective-permute-start.8
